TPU v7x, 512 devices: a whole 4x4x16 slice. The times are simulated.
512 devices in a mesh: ctx: 32 (over x, z_lo, core), tp: 16 (over y, z_hi).
Axes of the slice: x: 4, y: 4, z: 16 (z_hi: 4, z_lo: 4; z = z_hi * 4 + z_lo), core: 2. Of those that a mesh axis runs over, the one named last changes fastest.
Arguments:
- queries: bfloat16 [8192, 4096], P('ctx', 'tp'), may hold values from -6 to 6
- keys: bfloat16 [8192, 512], P('ctx'), may hold values from -6 to 6
- values: bfloat16 [8192, 512], P('ctx'), may hold values from -6 to 6
- out_weight: bfloat16 [4096, 8192], P('tp'), may hold values from -0.125 to 0.125
- storm_mask: int32 [64, 64], replicated, may hold values from 0 to 1, as said below
Outputs:
- mixed: bfloat16 [8192, 8192], P('ctx', 'tp')
Inputs may be any that keep to these rules, and one draw needn't show every extreme that they name: storm_mask[i, j] is 0 where j > i and 1 where 0 <= i - j < 4.
All inputs are finite; a program needn't handle non-finite values.
Results may differ from a plain program's by a relative error of at most 0.019.
Values may be sent and summed in bfloat16 or wider, within the bound.
A program may use at most 64 MiB of HBM per device.

v0:
```python
import jax
import jax.numpy as jnp
from jax import lax
from jax.sharding import PartitionSpec as P

HDIM = 128
BLOCK = 128
GQ = 8


def rows_of_mask(index_of_block, storm_mask):
    blocks = storm_mask.shape[0]
    one_hot = (index_of_block[:, None] == jnp.arange(blocks)[None, :]).astype(jnp.float32)
    return jnp.dot(one_hot, storm_mask.astype(jnp.float32))


def update(carry, query, keys_part, values_part, first, row_mask):
    count = keys_part.shape[0]
    blocks = row_mask.shape[1]
    block_of = (first + jnp.arange(count)) // BLOCK
    one_hot = (jnp.arange(blocks)[:, None] == block_of[None, :]).astype(jnp.float32)
    allowed = jnp.dot(row_mask, one_hot) > 0.5

    def compute(state):
        maximum, total, running_total = state
        scores = jnp.einsum(
            "qhd,kd->hqk", query, keys_part, preferred_element_type=jnp.float32
        ) * HDIM ** (-0.5)
        scores = jnp.where(allowed[None], scores, -1e30)
        peak = jnp.maximum(maximum, jnp.max(scores, axis=2))
        weights = jnp.where(allowed[None], jnp.exp(scores - peak[:, :, None]), 0.0)
        factor = jnp.exp(maximum - peak)
        total = total * factor + jnp.sum(weights, axis=2)
        running_total = running_total * factor[:, :, None] + jnp.einsum(
            "hqk,kd->hqd",
            weights.astype(jnp.bfloat16),
            values_part,
            preferred_element_type=jnp.float32,
        )
        return (peak, total, running_total)

    return lax.cond(jnp.any(allowed), compute, lambda state: state, carry)


def body(queries, keys, values, out_weight, storm_mask):
    rows, width = queries.shape
    heads = width // HDIM
    place = lax.axis_index("ctx")
    shared_head = lax.axis_index("tp") * heads // GQ
    local_keys = lax.dynamic_slice_in_dim(keys, shared_head * HDIM, HDIM, 1)
    own_values = lax.dynamic_slice_in_dim(values, shared_head * HDIM, HDIM, 1)
    per_device = rows // BLOCK
    owned = place * per_device + jnp.arange(per_device)
    row_mask = jnp.repeat(rows_of_mask(owned, storm_mask), BLOCK, axis=0)
    query = queries.reshape(rows, heads, HDIM)
    initial = (
        jnp.full((heads, rows), -1e30, jnp.float32),
        jnp.zeros((heads, rows), jnp.float32),
        jnp.zeros((heads, rows, HDIM), jnp.float32),
    )
    carry = initial
    keys_part = lax.all_gather(local_keys, "ctx", axis=0, tiled=True)
    values_part = lax.all_gather(own_values, "ctx", axis=0, tiled=True)
    count = keys_part.shape[0]
    stride = 512

    def inner(state, number):
        first = number * stride
        keys_block = lax.dynamic_slice_in_dim(keys_part, first, stride, 0)
        values_block = lax.dynamic_slice_in_dim(values_part, first, stride, 0)
        return (update(state, query, keys_block, values_block, first, row_mask), None)

    carry, unused = lax.scan(inner, carry, jnp.arange(count // stride))
    maximum, total, running_total = carry
    attended = (
        (running_total / total[:, :, None])
        .astype(jnp.bfloat16)
        .transpose(1, 0, 2)
        .reshape(rows, width)
    )
    columns = out_weight.shape[1] // lax.axis_size("tp")
    whole = lax.psum(
        jnp.dot(attended, out_weight, preferred_element_type=jnp.float32).astype(jnp.bfloat16), "tp"
    ).astype(jnp.float32)
    result = lax.dynamic_slice_in_dim(whole, lax.axis_index("tp") * columns, columns, 1).astype(
        jnp.bfloat16
    )
    return result


def solution(mesh):
    placed = (P("ctx", "tp"), P("ctx", None), P("ctx", None), P("tp", None), P())
    return jax.shard_map(
        body, mesh=mesh, in_specs=placed, out_specs=P("ctx", "tp"), check_vma=False
    )
```

profile of v0, /device:TPU:1, one launch (start us, length us, event | category | flops | bytes accessed | tf_op | source)
XLA Modules:
  0.0 652.2 jit_solution(2344125904926054323)
XLA Ops:
  8.2 1.5 constant_dynamic-slice_fusion
  9.7 1.0 copy.8
  11.8 68.1 %all-gather.3.cloned.1.call-done = bf16[8192,128]{1,0:T(8,128)(2,1)} async-done(((bf16[256,128]{1,0:T(8,128)(2,1)}), bf16[8192,128]{1,0:T(8,128)(2,1)}) %all-gather.3.cloned.1.call-update) | async-done | bytes 2097168 | tf_op jit(solution)/shard_map/all_gather | solution.py:62
  80.0 66.0 %all-gather.5.cloned.1.call-done = bf16[8192,128]{1,0:T(8,128)(2,1)} async-done(((bf16[256,128]{1,0:T(8,128)(2,1)}), bf16[8192,128]{1,0:T(8,128)(2,1)}) %all-gather.5.cloned.1.call-update) | async-done | bytes 2097168 | tf_op jit(solution)/shard_map/all_gather | solution.py:63
  146.0 49.4 %while.17 = (s32[]{:T(128)}, f32[2,256]{1,0:T(2,128)S(1)}, f32[2,256]{1,0:T(2,128)S(1)}, f32[2,256,128]{2,1,0:T(8,128)S(1)}, s32[16]{0:T(128)S(1)}, /*index=5*/b...) while((s32[]{:T(128)}, f32[2,256]{1,0:T(2,128)S(1)}, ...), condition=%wide.region_6.7_spmd.clone, body=%wide.region_0.6_spmd.clone.sunk | while | flops 153822208 | bytes 4690489 | solution.py:73
  147.3 1.0 fusion.37
  148.9 3.0 conditional.3
  148.9 1.2 fusion.28
  150.4 1.4 convolution_add_fusion
  153.1 1.0 fusion.37
  156.0 1.0 fusion.37
  158.9 1.0 fusion.37
  161.9 1.0 fusion.37
  164.8 1.0 fusion.37
  167.7 1.0 fusion.37
  170.6 1.0 fusion.37
  173.5 1.0 fusion.37
  179.3 1.0 fusion.37
  182.2 1.0 fusion.37
  185.1 1.0 fusion.37
  188.0 1.0 fusion.37
  195.6 5.4 convolution_convert_fusion
  201.1 442.9 %all-reduce.2.cloned.1.call-done = bf16[256,8192]{1,0:T(8,128)(2,1)} async-done(((bf16[256,8192]{1,0:T(8,128)(2,1)}), bf16[256,8192]{1,0:T(8,128)(2,1)}) %all-reduce.2.cloned.1.call-update) | async-done | bytes 4194320 | tf_op jit(solution)/shard_map/psum | solution.py:82
  644.0 1.7 convert_convert_fusion
  (88 shorter events, 16.1 us)
Async XLA Ops:
  6.5 1.0 copy-start
  6.5 73.4 %all-gather.3.cloned.1.call-start = ((), (), s32[]{:S(2)}) async-start(), calls=%async_computation | async-start | bytes 2162688 | tf_op jit(solution)/shard_map/all_gather | solution.py:62
  8.1 137.8 %all-gather.5.cloned.1.call-start = ((), (), s32[]{:S(2)}) async-start(), calls=%async_computation.1 | async-start | bytes 2162688 | tf_op jit(solution)/shard_map/all_gather | solution.py:63
  9.7 634.3 %all-reduce.2.cloned.1.call-start = ((), (), s32[]{:S(2)}) async-start(), calls=%async_computation.2 | async-start | bytes 8388608 | tf_op jit(solution)/shard_map/psum | solution.py:82
Sparse Core Ops, SparseCore 0:
  9.5 70.4 all-gather.2
  82.1 63.8 all-gather.4
  201.2 442.7 all-reduce.1
where the time goes:
time: 658 us; the launch traced here: 652 us
  waiting for transfers between devices  577 us (88%)
  matrix products  24.8 us (4%)
  loops' own time  21.1 us (3%)
  local copies, waits for them, and re-layouts  13.9 us (2%)
  between operations  13.2 us (2%)
    psum x1, waiting for transfers between devices, body(): lax.psum(jnp.dot(attended, out_weight, preferred_element_type=jnp.float32...  443 us
    all_gather x1, waiting for transfers between devices, body(): keys_part = lax.all_gather(local_keys, 'ctx', axis=0, tiled=True)  68.1 us
    all_gather x1, waiting for transfers between devices, body(): values_part = lax.all_gather(own_values, 'ctx', axis=0, tiled=True)  66 us
    another operation x1, loops' own time, body(): carry, unused = lax.scan(inner, carry, jnp.arange(count // stride))  20.9 us
    dot_general x16, matrix products, update(): allowed = jnp.dot(row_mask, one_hot) > 0.5  15.7 us
  transfers between devices with their start and end apart: 3, of which 3 were waited for; matrix products, arithmetic and copies ran while one was open for 1% of the time, Pallas kernels for 0%

commit v1 on v0

v1 whole, which is shorter than its diff:
```python
import functools

import jax
import jax.numpy as jnp
from jax import lax
from jax.experimental import pallas as pl
from jax.experimental.pallas import tpu as pltpu
from jax.sharding import PartitionSpec as P

HDIM = 128
BLOCK = 128
MESH = pl.DeviceIdType.MESH
F32 = jnp.float32
BF16 = jnp.bfloat16
SCALE2 = HDIM ** (-0.5) * 1.4426950408889634
ORDER = ((0, 0), (-1, 0), (1, 0), (0, -1), (0, 1), (2, 0), (0, 2), (-1, -1), (-1, 1), (1, -1), (1, 1),
         (2, -1), (2, 1), (-1, 2), (1, 2), (2, 2))
KV_SENDS = 72
W_SLOTS = (10, 14)


def kernel(q_hbm, k_hbm, v_hbm, w_hbm, mask_ref, out_ref, qs, kv, wbuf, abuf, m_ref, acc_ref,
           ys2, ysp, ysm, yrel, yin, yacc, yown,
           local_sem, kv_send, kv_recv, kv_sib, w_send, wz_recv, wx_recv, wx_sib,
           a_send, a_recv, y_send, y_rel_recv, y_recv):
    ctx, tp = lax.axis_index("ctx"), lax.axis_index("tp")
    x, zl, core = ctx // 8, (ctx // 2) % 4, ctx % 2
    y, zh = tp // 4, tp % 4
    z = zh * 4 + zl

    def at_x(d):
        return (((x + d + 4) % 4) * 8 + zl * 2 + core, tp)

    def at_z(d):
        zz = (z + d + 16) % 16
        return (x * 8 + (zz % 4) * 2 + core, y * 4 + zz // 4)

    def at_y(d):
        return (ctx, ((y + d + 4) % 4) * 4 + zh)

    sibling = (x * 8 + zl * 2 + (1 - core), tp)
    devices = {"x+": at_x(1), "x-": at_x(-1), "z+": at_z(1), "z-": at_z(-1), "s": sibling,
               "y+": at_y(1), "y-": at_y(-1), "h+": at_z(4), "h-": at_z(-4), "f+": at_z(5), "f-": at_z(-5)}

    def remote(src, dst, ssem, rsem, to):
        return pltpu.make_async_remote_copy(src_ref=src, dst_ref=dst, send_sem=ssem, recv_sem=rsem,
                                            device_id=devices[to], device_id_type=MESH)

    def group_of(dx, dz):
        return ((x + dx + 4) % 4) * 4 + (zl + dz + 4) % 4

    own_group = x * 4 + zl

    local = []

    def load(src, dst):
        copy = pltpu.make_async_copy(src, dst, local_sem.at[len(local)])
        copy.start()
        local.append(copy)
        return copy

    head = pl.ds(pl.multiple_of(y * HDIM, HDIM), HDIM)
    own_kv = []
    for typ in range(2):
        rows = pl.ds(typ * BLOCK, BLOCK)
        own_kv.append((load(k_hbm.at[rows, head], kv.at[own_group, core * 2 + typ, 0]),
                       load(v_hbm.at[rows, head], kv.at[own_group, core * 2 + typ, 1])))
    q_loads = [load(q_hbm.at[pl.ds(b * BLOCK, BLOCK), pl.ds(h * HDIM, HDIM)], qs.at[b, pl.ds(h * HDIM, HDIM)])
               for b in range(2) for h in range(2)]

    def w_columns(yy, zz):
        return pl.ds(pl.multiple_of((yy * 4 + zz) * 512, 512), 512)

    w_loads = [load(w_hbm.at[:, w_columns(yy, zh)], wbuf.at[zh, yy]) for yy in range(4)]

    barrier = pltpu.get_barrier_semaphore()
    for device in devices.values():
        pl.semaphore_signal(barrier, inc=1, device_id=device, device_id_type=MESH)
    pl.semaphore_wait(barrier, len(devices))

    sends = []

    shift = {"x+": (-1, 0), "x-": (1, 0), "z+": (0, -1), "z-": (0, 1)}
    count = [0]

    def kv_ref(typ, dx, dz, part, which=None):
        ref = kv.at[group_of(dx, dz), (core if which is None else which) * 2 + typ]
        return ref if part is None else ref.at[part]

    def kv_forward(typ, dx, dz, part, to):
        number = count[0]
        count[0] += 1

        def copy():
            ref = kv_ref(typ, dx, dz, part)
            if to == "s":
                rsem = kv_sib.at[typ, dx % 4, dz % 4]
            else:
                sx, sz = shift[to]
                rsem = kv_recv.at[typ, (dx + sx) % 4, (dz + sz) % 4, part or 0]
            return remote(ref, ref, kv_send.at[number], rsem, to)

        copy().start()
        sends.append(lambda: copy().wait_send())

    def kv_handle(dx, dz):
        for typ in range(2):
            along = (dx, dz) if typ == 0 else (dz, dx)
            one, two = ("x", "z") if typ == 0 else ("z", "x")
            if (dx, dz) == (0, 0):
                for part in range(2):
                    own_kv[typ][part].wait()
            else:
                last = along[1] if along[1] != 0 else along[0]
                parts = (0, 1) if last == 2 else (None,)
                for part in parts:
                    ref = kv_ref(typ, dx, dz, part)
                    remote(ref, ref, kv_send.at[0], kv_recv.at[typ, dx % 4, dz % 4, part or 0], "s").wait_recv()
            if along[1] == 0:
                if along[0] == 0:
                    kv_forward(typ, dx, dz, None, one + "+")
                    kv_forward(typ, dx, dz, None, one + "-")
                elif along[0] == -1:
                    kv_forward(typ, dx, dz, 0, one + "+")
                elif along[0] == 1:
                    kv_forward(typ, dx, dz, 1, one + "-")
                kv_forward(typ, dx, dz, None, two + "+")
                kv_forward(typ, dx, dz, None, two + "-")
            elif along[1] == -1:
                kv_forward(typ, dx, dz, 0, two + "+")
            elif along[1] == 1:
                kv_forward(typ, dx, dz, 1, two + "-")
        for typ in range(2):
            kv_forward(typ, dx, dz, None, "s")

    row0 = pl.multiple_of(core * 128, 128)
    w_rows = {"all": pl.ds(row0, 128), "low": pl.ds(row0, 64), "high": pl.ds(pl.multiple_of(row0 + 64, 64), 64)}
    w_count = [0]

    def w_send_sem():
        w_count[0] += 1
        return w_send.at[w_count[0] - 1]

    def w_ref(dzh, dx, rows):
        return wbuf.at[(zh + dzh + 4) % 4, (x + dx + 4) % 4, w_rows[rows]]

    w_dirs = {"+": (1, "low", 0, 3), "-": (-1, "high", 2, 0)}
    w_sems = {}
    for name in w_dirs:
        w_sems[name] = (w_send_sem(), w_send_sem())

    def w_first(name):
        sign, far, slot, edge = w_dirs[name]

        @pl.when(zl == edge)
        def _():
            for part, (reach, rows, to) in enumerate(((1, "all", "z" + name), (2, far, "f" + name))):
                src = w_hbm.at[w_rows[rows], w_columns(x, (zh + sign * reach + 4) % 4)]
                remote(src, w_ref(0, 0, rows), w_sems[name][part], wz_recv.at[slot + part], to).start()

    def w_slot(name, k):
        sign, far, slot, edge = w_dirs[name]
        here = k if sign == 1 else 3 - k

        @pl.when(zl == here)
        def _():
            for part, (reach, rows) in enumerate(((1, "all"), (2, far))):
                ref = w_ref(-sign * reach, 0, rows)
                copy = remote(ref, ref, w_sems[name][part], wz_recv.at[slot + part], "z" + name)
                copy.wait_recv()
                if k < 3:
                    copy.start()

    def w_z_waits():
        for name in w_dirs:
            for part, rows in enumerate(("all", w_dirs[name][1])):
                ref = w_ref(1, 0, rows)
                copy = remote(ref, ref, w_sems[name][part], wz_recv.at[w_dirs[name][2] + part], "z" + name)
                copy.wait_send()

    def w_forward(dzh, dx, rows, to):
        ref = w_ref(dzh, dx, rows)
        if to == "s":
            rsem = wx_sib.at[dzh % 4, dx % 4]
        else:
            sx = shift[to][0]
            rsem = wx_recv.at[dzh % 4, (dx + sx) % 4, 1 if rows == "high" else 0]
        copy = remote(ref, ref, w_send_sem(), rsem, to)
        copy.start()
        sends.append(lambda: copy.wait_send())

    def w_wait(dzh, dx, rows):
        ref = w_ref(dzh, dx, rows)
        remote(ref, ref, w_send.at[0], wx_recv.at[dzh % 4, dx % 4, 1 if rows == "high" else 0], "s").wait_recv()

    zhs = (-1, 1, 2)

    def w_x1():
        for dzh in zhs:
            w_forward(dzh, 0, "all", "x+")
            w_forward(dzh, 0, "all", "x-")
        for dzh in zhs:
            w_forward(dzh, 0, "all", "s")

    def w_x2():
        for dzh in zhs:
            w_wait(dzh, -1, "all")
            w_forward(dzh, -1, "low", "x+")
            w_wait(dzh, 1, "all")
            w_forward(dzh, 1, "high", "x-")
            w_forward(dzh, -1, "all", "s")
            w_forward(dzh, 1, "all", "s")

    def w_x3():
        for dzh in zhs:
            w_wait(dzh, 2, "low")
            w_wait(dzh, 2, "high")
            w_forward(dzh, 2, "all", "s")

    other_rows = pl.ds(pl.multiple_of((1 - core) * 128, 128), 128)

    def w_x4():
        for dzh in zhs:
            for dx in (0, -1, 1, 2):
                ref = wbuf.at[(zh + dzh + 4) % 4, (x + dx + 4) % 4, other_rows]
                remote(ref, ref, w_send.at[0], wx_sib.at[dzh % 4, dx % 4], "s").wait_recv()

    m_ref[...] = jnp.full(m_ref.shape, -1e30, F32)
    acc_ref[...] = jnp.zeros(acc_ref.shape, F32)
    for copy in q_loads:
        copy.wait()
    ones = jnp.ones((512, HDIM), BF16)

    def attend(group):
        keys = kv[group, :, 0].reshape(512, HDIM)
        values = jnp.concatenate([kv[group, :, 1].reshape(512, HDIM), ones], axis=1)
        for b in range(2):
            scores = lax.dot_general(qs[b], keys, (((1,), (1,)), ((), ())), preferred_element_type=F32)
            parts = []
            for j in range(4):
                allowed = mask_ref[ctx * 2 + b, group * 4 + j].astype(F32)
                parts.append(scores[:, j * BLOCK:(j + 1) * BLOCK] * SCALE2 + (allowed - 1.0) * 1e30)
            top = jnp.maximum(jnp.maximum(parts[0], parts[1]), jnp.maximum(parts[2], parts[3]))
            old = m_ref[b]
            new = jnp.maximum(old, jnp.max(top, axis=1, keepdims=True))
            factor = jnp.exp2(old - new)
            weights = jnp.concatenate([jnp.exp2(part - new).astype(BF16) for part in parts], axis=1)
            m_ref[b] = new
            acc_ref[b] = acc_ref[b] * jnp.concatenate([factor, factor], axis=1) + jnp.dot(
                weights, values, preferred_element_type=F32)

    def pick(number, axis):
        value = 0
        for e, offset in enumerate(ORDER):
            if offset[axis] % 4:
                value = value + jnp.where(number == e, offset[axis] % 4, 0)
        return value

    def step(i, carry):
        for e, (dx, dz) in enumerate(ORDER):
            @pl.when(i == e)
            def _():
                kv_handle(dx, dz)
                if e == 0:
                    w_first("+")
                    w_first("-")
                for k, slot in enumerate(W_SLOTS):
                    if slot == e:
                        w_slot("+", k)
                        w_slot("-", k)

        @pl.when(i > 0)
        def _():
            dx, dz = pick(i - 1, 0), pick(i - 1, 1)
            group = ((x + dx) % 4) * 4 + (zl + dz) % 4
            for typ in range(2):
                ref = kv.at[group, (1 - core) * 2 + typ]
                remote(ref, ref, kv_send.at[0], kv_sib.at[typ, dx, dz], "s").wait_recv()

            @pl.when(group <= own_group)
            def _():
                attend(group)
        return carry

    lax.fori_loop(0, len(ORDER) + 1, step, 0)

    a_count = [0]

    def a_ref(dzh, b, part):
        ref = abuf.at[(zh + dzh + 4) % 4, b]
        return ref if part is None else ref.at[pl.ds(part * 64, 64)]

    def a_forward(dzh, b, part, to):
        ref = a_ref(dzh, b, part)
        there = dzh - 1 if to == "h+" else dzh + 1
        copy = remote(ref, ref, a_send.at[a_count[0]], a_recv.at[b, there % 4, part or 0], to)
        a_count[0] += 1
        copy.start()
        sends.append(lambda: copy.wait_send())

    def a_wait(dzh, b, part):
        ref = a_ref(dzh, b, part)
        remote(ref, ref, a_send.at[0], a_recv.at[b, dzh % 4, part or 0], "s").wait_recv()

    for b in range(2):
        done = (acc_ref[b, :, :HDIM] / acc_ref[b, :, HDIM:]).astype(BF16)
        abuf[zh, b] = jnp.concatenate([done[:BLOCK], done[BLOCK:]], axis=1)
        a_forward(0, b, None, "h+")
        a_forward(0, b, None, "h-")

    for k in range(len(W_SLOTS), 4):
        w_slot("+", k)
        w_slot("-", k)
    w_x1()
    for b in range(2):
        a_wait(-1, b, None)
        a_forward(-1, b, 0, "h+")
        a_wait(1, b, None)
        a_forward(1, b, 1, "h-")
    w_x2()
    w_x3()
    w_x4()
    for copy in w_loads:
        copy.wait()

    y_count = [0]

    def y_forward(src, dst, rsem, to):
        copy = remote(src, dst, y_send.at[y_count[0]], rsem, to)
        y_count[0] += 1
        copy.start()
        sends.append(lambda: copy.wait_send())

    def project(b, dy):
        yy = (y + dy + 4) % 4
        total = jnp.dot(abuf[0, b], wbuf[0, yy], preferred_element_type=F32)
        for zz in range(1, 4):
            total = total + jnp.dot(abuf[zz, b], wbuf[zz, yy], preferred_element_type=F32)
        return total

    for b in range(2):
        a_wait(2, b, 0)
        a_wait(2, b, 1)
        far = project(b, 2).astype(BF16)
        for half in range(2):
            ys2[b, half] = far[:, half * 256:(half + 1) * 256]
            y_forward(ys2.at[b, half], yrel.at[b, half], y_rel_recv.at[b, half], "y+" if half == 0 else "y-")
        up = project(b, 1)
        ysp[b, 1] = up[:, 256:].astype(BF16)
        yacc[b, 0] = up[:, :256]
        y_forward(ysp.at[b, 1], yin.at[b, 0, 1], y_recv.at[b, 0, 1], "y+")
        down = project(b, -1)
        ysm[b, 0] = down[:, :256].astype(BF16)
        yacc[b, 1] = down[:, 256:]
        y_forward(ysm.at[b, 0], yin.at[b, 1, 0], y_recv.at[b, 1, 0], "y-")
        yown[b] = project(b, 0)
    for b in range(2):
        for half, sent, to in ((0, ysp, "y+"), (1, ysm, "y-")):
            remote(ys2.at[b, half], yrel.at[b, half], y_send.at[0], y_rel_recv.at[b, half], to).wait_recv()
            sent[b, half] = (yacc[b, half] + yrel[b, half].astype(F32)).astype(BF16)
            y_forward(sent.at[b, half], yin.at[b, half, half], y_recv.at[b, half, half], to)
    for b in range(2):
        for half in range(2):
            for side in range(2):
                remote(ys2.at[b, half], yin.at[b, side, half], y_send.at[0], y_recv.at[b, side, half], "s").wait_recv()
            columns = pl.ds(half * 256, 256)
            out_ref[pl.ds(b * BLOCK, BLOCK), columns] = (
                yown[b, :, columns] + yin[b, 0, half].astype(F32) + yin[b, 1, half].astype(F32)).astype(BF16)

    for wait in sends:
        wait()
    w_z_waits()


def body(queries, keys, values, out_weight, storm_mask):
    rows, width = queries.shape
    anywhere = pl.BlockSpec(memory_space=pl.ANY)
    dma = pltpu.SemaphoreType.DMA
    return pl.pallas_call(
        kernel,
        out_shape=jax.ShapeDtypeStruct((rows, 512), BF16),
        in_specs=[anywhere, anywhere, anywhere, anywhere, pl.BlockSpec(memory_space=pltpu.SMEM)],
        out_specs=pl.BlockSpec(memory_space=pltpu.VMEM),
        scratch_shapes=[
            pltpu.VMEM((2, 256, HDIM), BF16),
            pltpu.VMEM((16, 4, 2, BLOCK, HDIM), BF16),
            pltpu.VMEM((4, 4, 256, 512), BF16),
            pltpu.VMEM((4, 2, BLOCK, 256), BF16),
            pltpu.VMEM((2, 256, HDIM), F32),
            pltpu.VMEM((2, 256, 256), F32),
            pltpu.VMEM((2, 2, BLOCK, 256), BF16),
            pltpu.VMEM((2, 2, BLOCK, 256), BF16),
            pltpu.VMEM((2, 2, BLOCK, 256), BF16),
            pltpu.VMEM((2, 2, BLOCK, 256), BF16),
            pltpu.VMEM((2, 2, 2, BLOCK, 256), BF16),
            pltpu.VMEM((2, 2, BLOCK, 256), F32),
            pltpu.VMEM((2, BLOCK, 512), F32),
            dma((12,)), dma((KV_SENDS,)), dma((2, 4, 4, 2)), dma((2, 4, 4)),
            dma((28,)), dma((4,)), dma((4, 4, 2)), dma((4, 4)),
            dma((8,)), dma((2, 4, 2)), dma((12,)), dma((2, 2)), dma((2, 2, 2)),
        ],
        compiler_params=pltpu.CompilerParams(
            collective_id=0, has_side_effects=True, vmem_limit_bytes=56 * 1024 * 1024),
    )(queries, keys, values, out_weight, storm_mask)


def solution(mesh):
    placed = (P("ctx", "tp"), P("ctx", None), P("ctx", None), P("tp", None), P())
    return jax.shard_map(
        body, mesh=mesh, in_specs=placed, out_specs=P("ctx", "tp"), check_vma=False
    )
```

time: 658 us -> 97.8 us (0.15)
  waiting for transfers between devices: 577 us -> 0 us
  Pallas kernels: 0 us -> 95.9 us
  matrix products: 24.8 us -> 0 us
  loops' own time: 21.1 us -> 0 us
  between operations: 13.2 us -> 0.01 us
  local copies, waits for them, and re-layouts: 13.9 us -> 1.67 us
    psum x1 -> x0, waiting for transfers between devices: 443 us -> none  [body(): lax.psum(jnp.dot(attended, out_weight, preferred_element_type=jnp.float32...]
    all_gather x2 -> x0, waiting for transfers between devices: 134 us -> none  [the longest x1 68.1 us: body(): keys_part = lax.all_gather(local_keys, 'ctx', axis=0, tiled=True)]
    pallas_call x0 -> x1, Pallas kernels: none -> 95.9 us  [body(): pl.pallas_call(kernel, out_shape=jax.ShapeDtypeStruct((rows, 512), BF16),...]
    dot_general x20 -> x0, matrix products: 24.8 us -> none  [the longest x16 15.7 us: update(): allowed = jnp.dot(row_mask, one_hot) > 0.5]
    another operation x17 -> x0, loops' own time: 21.1 us -> none  [the longest x1 20.9 us: body(): carry, unused = lax.scan(inner, carry, jnp.arange(count // stride))]
    dynamic_slice x18 -> x0, local copies, waits for them, and re-layouts: 11.5 us -> none  [the longest x16 9.38 us: body(): carry, unused = lax.scan(inner, carry, jnp.arange(count // stride))]
  transfers between devices with their start and end apart: 3 -> 0, of which waited for: 3 -> 0; matrix products, arithmetic and copies ran while one was open for 1% -> 0% of each run, Pallas kernels for 0% -> 0%
where the time goes in v1:
time: 97.8 us; the launch traced here: 97.6 us
  Pallas kernels  95.9 us (98%)
  local copies, waits for them, and re-layouts  1.67 us (2%)
    pallas_call x1, Pallas kernels, body(): pl.pallas_call(kernel, out_shape=jax.ShapeDtypeStruct((rows, 512), BF16),...  95.9 us

profile of v1, /device:TPU:1, one launch (start us, length us, event | category | flops | bytes accessed | tf_op | source)
XLA Modules:
  0.0 97.6 jit_solution(3224863777452747172)
XLA Ops:
  0.0 95.9 %shard_map.55 = bf16[256,512]{1,0:T(8,128)(2,1)} custom-call(bf16[256,256]{1,0:T(8,128)(2,1)} %q_hbm.1, bf16[256,512]{1,0:T(8,128)(2,1)} %k_hbm.1, bf16[256,512]{1,0:T(8,128)(2,1)} %v_hbm.1, bf16[256,8192]{1,0:T(8,128)(2,1)} %w_hbm.1, s32[64,64]{1,0:T(8,128)} %mask_ref.1), custom_call_target="tpu_custom_call" | custom-call | tf_op jit(solution)/shard_map/pallas_call | solution.py:379
  95.9 1.7 %copy.7 = bf16[256,512]{1,0:T(8,128)(2,1)} copy(bf16[256,512]{1,0:T(8,128)(2,1)} %shard_map.55) | data formatting | bytes 524288

commit v2 on v0

v2 whole, which is shorter than its diff:
```python
import functools

import jax
import jax.numpy as jnp
from jax import lax
from jax.experimental import pallas as pl
from jax.experimental.pallas import tpu as pltpu
from jax.sharding import PartitionSpec as P

HDIM = 128
BLOCK = 128
MESH = pl.DeviceIdType.MESH
F32 = jnp.float32
BF16 = jnp.bfloat16
SCALE2 = HDIM ** (-0.5) * 1.4426950408889634
PROGRAM = (
    ((0, 0), ()),
    ((0, -1), ((0, -1, 0), (0, 1, 0), (0, 0, -1), (0, 0, 1), (1, 0, -1), (1, 0, 1), (0, 2, 0), (1, -1, 0), (1, 1, 0), (1, 0, 2), (2, -1, 0), (2, 1, 0), (2, 0, -1), (2, 0, 1), (3, 0, -1), (3, 0, 1), (2, 2, 0), (3, -1, 0), (3, 1, 0))),
    ((0, 1), ((3, 0, 2), (0, -1, -1), (0, -1, 1), (1, -1, -1), (1, 1, -1))),
    ((-1, 0), ((0, 1, -1), (0, 1, 1), (1, -1, 1), (1, 1, 1))),
    ((1, 0), ((0, 0, 2), (1, 2, 0))),
    ((-1, -1), ((0, 2, -1), (0, 2, 1), (1, -1, 2), (1, 1, 2), (2, -1, -1), (2, -1, 1), (3, -1, -1), (3, 1, -1), (2, 1, -1), (2, 1, 1), (3, -1, 1), (3, 1, 1), (2, 0, 2), (3, 2, 0))),
    ((1, -1), ((2, 2, -1), (2, 2, 1), (3, -1, 2), (3, 1, 2))),
    ((-1, 1), ((0, -1, 2), (1, 2, -1))),
    ((1, 1), ((0, 1, 2), (1, 2, 1), (0, 2, 2), (1, 2, 2))),
    ((0, 2), ((2, -1, 2), (3, 2, -1))),
    ((2, 0), ((2, 1, 2), (3, 2, 1))),
    ((-1, 2), ((2, 2, 2), (3, 2, 2))),
    ((2, -1), ()),
    ((1, 2), ()),
    ((2, 1), ()),
    ((2, 2), ()),
)
FIRST = (0, 1, 0, 1)
SUB = 64
W_SLOTS = (1, 3, 5, 7, 10, 13)
W_EARLY = 3


def kernel(q_hbm, k_hbm, v_hbm, w_hbm, mask_hbm, out_ref, mask_ref, qs, kv, wbuf, abuf, m_ref, acc_ref,
           ysend, yin, total,
           local_sem, kv_send, kv_recv, kv_sib, w_send, wz_recv, wx_recv, wx_sib,
           a_send, a_recv, y_send, y_recv):
    ctx, tp = lax.axis_index("ctx"), lax.axis_index("tp")
    x, zl, core = ctx // 8, (ctx // 2) % 4, ctx % 2
    y, zh = tp // 4, tp % 4
    z = zh * 4 + zl

    def at_x(d):
        return (((x + d + 4) % 4) * 8 + zl * 2 + core, tp)

    def at_z(d):
        zz = (z + d + 16) % 16
        return (x * 8 + (zz % 4) * 2 + core, y * 4 + zz // 4)

    def at_y(d):
        return (ctx, ((y + d + 4) % 4) * 4 + zh)

    devices = {"x+": at_x(1), "x-": at_x(-1), "x2": at_x(2), "z+": at_z(1), "z-": at_z(-1), "z2": at_z(2),
               "back": at_z(-2), "s": (x * 8 + zl * 2 + (1 - core), tp), "y+": at_y(1), "y-": at_y(-1), "y2": at_y(2),
               "h+": at_z(4), "h-": at_z(-4), "f+": at_z(5), "f-": at_z(-5)}

    def remote(src, dst, ssem, rsem, to):
        return pltpu.make_async_remote_copy(src_ref=src, dst_ref=dst, send_sem=ssem, recv_sem=rsem,
                                            device_id=devices[to], device_id_type=MESH)

    def group_of(dx, dz):
        return ((x + dx + 4) % 4) * 4 + (zl + dz + 4) % 4

    own_group = x * 4 + zl

    def load(src, dst, kind):
        pltpu.make_async_copy(src, dst, local_sem.at[kind]).start()

    def loaded(whole, kind):
        pltpu.make_async_copy(whole, whole, local_sem.at[kind]).wait()

    def kv_at(group, which, sub):
        return ((group * 2 + which) * 4 + sub) * 2

    head = pl.ds(pl.multiple_of(y * HDIM, HDIM), HDIM)
    for sub in range(4):
        rows = pl.ds(sub * SUB, SUB)
        load(k_hbm.at[rows, head], kv.at[kv_at(own_group, core, sub)], sub)
        load(v_hbm.at[rows, head], kv.at[kv_at(own_group, core, sub) + 1], sub)
    for b in range(2):
        for h in range(2):
            load(q_hbm.at[pl.ds(b * BLOCK, BLOCK), pl.ds(h * HDIM, HDIM)], qs.at[pl.ds((b * 2 + h) * HDIM, HDIM)], 4)

    def w_columns(yy, zz):
        return pl.ds(pl.multiple_of((yy * 4 + zz) * 512, 512), 512)

    load(mask_hbm, mask_ref, 5)
    for yy in range(4):
        load(w_hbm.at[:, w_columns(yy, zh)], wbuf.at[zh, yy], 6)

    barrier = pltpu.get_barrier_semaphore()
    for device in devices.values():
        pl.semaphore_signal(barrier, inc=1, device_id=device, device_id_type=MESH)
    pl.semaphore_wait(barrier, len(devices))

    shift = {"x+": (-1, 0), "x-": (1, 0), "x2": (2, 0), "z+": (0, -1), "z-": (0, 1), "z2": (0, 2)}
    count = [0]

    def kv_ref(sub, dx, dz, part):
        first = kv_at(group_of(dx, dz), core, sub)
        return kv.at[pl.ds(first, 2)] if part is None else kv.at[pl.ds(first + part, 1)]

    def kv_forward(sub, dx, dz, part, to):
        ref = kv_ref(sub, dx, dz, part)
        count[0] += 2 if part is None else 1
        if to == "s":
            rsem = kv_sib.at[dx % 4, dz % 4]
        else:
            sx, sz = shift[to]
            rsem = kv_recv.at[sub, (dx + sx) % 4, (dz + sz) % 4]
        remote(ref, ref, kv_send, rsem, to).start()

    def kv_handle(sub, dx, dz):
        along = (dx, dz) if FIRST[sub] == 0 else (dz, dx)
        one, two = ("x", "z") if FIRST[sub] == 0 else ("z", "x")
        if (dx, dz) == (0, 0):
            loaded(kv_ref(sub, 0, 0, None), sub)
        else:
            ref = kv_ref(sub, dx, dz, None)
            remote(ref, ref, kv_send, kv_recv.at[sub, dx % 4, dz % 4], "s").wait_recv()
        if along[1] == 0:
            if along[0] == 0:
                kv_forward(sub, dx, dz, None, one + "+")
                kv_forward(sub, dx, dz, None, one + "-")
                kv_forward(sub, dx, dz, None, one + "2")
            kv_forward(sub, dx, dz, None, two + "+")
            kv_forward(sub, dx, dz, None, two + "-")
        elif along[1] == -1:
            kv_forward(sub, dx, dz, 0, two + "+")
        elif along[1] == 1:
            kv_forward(sub, dx, dz, 1, two + "-")
        kv_forward(sub, dx, dz, None, "s")

    row0 = core * 128
    w_dirs = {"+": (1, ((1, 0), (1, 64), (2, 0))), "-": (-1, ((1, 0), (1, 64), (2, 64)))}
    w_pieces = [(name, j) for j in range(3) for name in w_dirs]
    w_index = {piece: n for n, piece in enumerate(w_pieces)}

    def w_ref(name, j, dx, part=None, own=False, other=False):
        sign, pieces = w_dirs[name]
        reach, first = pieces[j]
        rows, size = ((1 - core) * 128 if other else row0) + first, 64
        if part is not None:
            rows, size = rows + part * 32, 32
        source = zh if own else (zh - sign * reach + 4) % 4
        return wbuf.at[source, (x + dx + 4) % 4, pl.ds(pl.multiple_of(rows, 32), size)]

    def w_first():
        for name, j in w_pieces:
            sign, pieces = w_dirs[name]
            reach, first = pieces[j]

            @pl.when(zl == (3 if sign == 1 else 0))
            def _():
                src = w_hbm.at[pl.ds(pl.multiple_of(row0 + first, 64), 64), w_columns(x, (zh + sign * reach + 4) % 4)]
                remote(src, w_ref(name, j, 0, own=True), w_send, wz_recv.at[w_index[name, j]],
                       ("z" if reach == 1 else "f") + name).start()

    def w_place(name, number):
        return zl == (number if name == "+" else 3 - number)

    def w_slot(s, then=False):
        for name, j in w_pieces:
            number = s - j
            if 0 <= number <= 3:
                @pl.when(w_place(name, number))
                def _():
                    ref = w_ref(name, j, 0)
                    copy = remote(ref, ref, w_send, wz_recv.at[w_index[name, j]], "z" + name)
                    copy.wait_recv()
                    if number < 3:
                        copy.start()
                    if then:
                        w_x1(name, j)

    def w_x1_copy(name, j, to):
        ref = w_ref(name, j, 0)
        n = w_index[name, j]
        rsem = wx_sib if to == "s" else wx_recv.at[n, shift[to][0] % 4 - 1]
        return remote(ref, ref, w_send, rsem, to)

    def w_x1(name, j):
        for to in ("x+", "x-", "s"):
            w_x1_copy(name, j, to).start()

    def w_x1_early():
        for name, j in w_pieces:
            numbers = [number for number in range(4) if number + j < W_EARLY]
            if len(numbers) == 4:
                w_x1(name, j)
            elif numbers:
                @pl.when(zl < len(numbers) if name == "+" else zl > 3 - len(numbers))
                def _():
                    w_x1(name, j)

    def w_forward(name, j, dx, part, to):
        ref = w_ref(name, j, dx, part)
        n = w_index[name, j]
        rsem = wx_sib if to == "s" else wx_recv.at[n, (dx + shift[to][0]) % 4 - 1]
        remote(ref, ref, w_send, rsem, to).start()

    def w_wait(name, j, dx):
        ref = w_ref(name, j, dx)
        remote(ref, ref, w_send, wx_recv.at[w_index[name, j], dx % 4 - 1], "s").wait_recv()

    def w_x2(name, j):
        w_wait(name, j, -1)
        w_forward(name, j, -1, 0, "x+")
        w_wait(name, j, 1)
        w_forward(name, j, 1, 1, "x-")
        w_forward(name, j, -1, None, "s")
        w_forward(name, j, 1, None, "s")

    def w_x3(name, j):
        w_wait(name, j, 2)
        w_forward(name, j, 2, None, "s")

    def w_x4():
        ref = wbuf.at[pl.ds(0, 3), pl.ds(0, 2)]
        remote(ref, ref, w_send, wx_sib, "s").wait_recv()

    m_ref[...] = jnp.full(m_ref.shape, -1e30, F32)
    acc_ref[...] = jnp.zeros(acc_ref.shape, F32)
    loaded(mask_ref, 5)
    loaded(qs, 4)
    ones = jnp.ones((512, HDIM), BF16)

    def attend(group):
        both = kv[pl.ds(group * 16, 16)].reshape(8, 2, SUB, HDIM)
        keys = both[:, 0].reshape(512, HDIM)
        values = jnp.concatenate([both[:, 1].reshape(512, HDIM), ones], axis=1)
        bias = [[(mask_ref[ctx * 2 + b, group * 4 + j].astype(F32) - 1.0) * 1e30 for j in range(4)] for b in range(2)]
        scores = [lax.dot_general(qs[n * 256:(n + 1) * 256], keys, (((1,), (1,)), ((), ())), preferred_element_type=F32)
                  for n in range(2)]
        for n in range(2):
            rows = slice(n * 256, (n + 1) * 256)
            parts = [scores[n][:, j * BLOCK:(j + 1) * BLOCK] * SCALE2 + bias[n * 256 // 256][j] for j in range(4)]
            top = jnp.maximum(jnp.maximum(parts[0], parts[1]), jnp.maximum(parts[2], parts[3]))
            old = m_ref[rows]
            new = jnp.maximum(old, jnp.max(top, axis=1, keepdims=True))
            factor = jnp.exp2(old - new)
            weights = jnp.concatenate([jnp.exp2(part - new).astype(BF16) for part in parts], axis=1)
            m_ref[rows] = new
            acc_ref[rows] = acc_ref[rows] * jnp.concatenate([factor, factor], axis=1) + jnp.dot(
                weights, values, preferred_element_type=F32)

    def pick(number, axis):
        value = 0
        for e, (offset, _) in enumerate(PROGRAM):
            if offset[axis] % 4:
                value = value + jnp.where(number == e, offset[axis] % 4, 0)
        return value

    for sub in range(4):
        kv_handle(sub, 0, 0)
    w_first()

    def step(i, carry):
        for e, (_, pieces) in enumerate(PROGRAM):
            if pieces or e in W_SLOTS:
                @pl.when(i == e)
                def _():
                    for piece in pieces:
                        kv_handle(*piece)
                    if e in W_SLOTS:
                        if W_SLOTS.index(e) == W_EARLY:
                            w_x1_early()
                        w_slot(W_SLOTS.index(e), then=W_SLOTS.index(e) >= W_EARLY)

        dx, dz = pick(i, 0), pick(i, 1)
        group = ((x + dx) % 4) * 4 + (zl + dz) % 4
        ref = kv.at[pl.ds(kv_at(group, 1 - core, 0), 8)]
        remote(ref, ref, kv_send, kv_sib.at[dx, dz], "s").wait_recv()

        @pl.when(group <= own_group)
        def _():
            attend(group)
        return carry

    lax.fori_loop(0, len(PROGRAM), step, 0)

    def a_ref(dzh, quarter, part):
        rows = (quarter % 2) * 64
        ref = abuf.at[(zh + dzh + 4) % 4, quarter // 2]
        return ref.at[pl.ds(rows, 64)] if part is None else ref.at[pl.ds(rows + part * 32, 32)]

    def a_forward(dzh, quarter, part, to):
        ref = a_ref(dzh, quarter, part)
        there = dzh - 1 if to == "h+" else dzh + 1
        remote(ref, ref, a_send, a_recv.at[quarter, there % 4 - 1], to).start()

    def a_wait(dzh, quarter):
        ref = a_ref(dzh, quarter, None)
        remote(ref, ref, a_send, a_recv.at[quarter, dzh % 4 - 1], "s").wait_recv()

    def a_direct(quarter):
        a_forward(0, quarter, None, "h+")
        a_forward(0, quarter, None, "h-")

    def a_relay(quarter):
        a_wait(-1, quarter)
        a_forward(-1, quarter, 0, "h+")
        a_wait(1, quarter)
        a_forward(1, quarter, 1, "h-")

    for b in range(2):
        rows = pl.ds(b * 256, 256)
        done = (acc_ref[rows, :HDIM] / acc_ref[rows, HDIM:]).astype(BF16)
        abuf[zh, b] = jnp.concatenate([done[:BLOCK], done[BLOCK:]], axis=1)
        a_direct(2 * b)
        a_direct(2 * b + 1)

    def project(dzh, half=None):
        zz = (zh + dzh + 4) % 4
        rows = slice(None) if half is None else slice(half * 128, half * 128 + 128)
        attended = abuf[zz].reshape(256, 256) if half is None else abuf[zz, half]
        for dy in range(4):
            part = jnp.dot(attended, wbuf[zz, (y + dy) % 4], preferred_element_type=F32)
            total[dy, rows] = part if half is None else total[dy, rows] + part

    def y_partial(half):
        a_wait(2, 2 * half)
        a_wait(2, 2 * half + 1)
        zz = (zh + 2) % 4
        rows = slice(half * 128, half * 128 + 128)
        for n, (dy, to) in enumerate(((2, "y2"), (1, "y+"), (3, "y-"), (0, None))):
            part = total[dy, rows] + jnp.dot(abuf[zz, half], wbuf[zz, (y + dy) % 4], preferred_element_type=F32)
            if to is None:
                total[dy, rows] = part
            else:
                ysend[half, n] = part.astype(BF16)
                remote(ysend.at[half, n], yin.at[half, n], y_send, y_recv.at[half, n], to).start()

    def y_sum(half):
        rows = slice(half * 128, half * 128 + 128)
        result = total[0, rows]
        for n in range(3):
            remote(ysend.at[half, n], yin.at[half, n], y_send, y_recv.at[half, n], "s").wait_recv()
            result = result + yin[half, n].astype(F32)
        out_ref[rows] = result.astype(BF16)

    def each(action, j):
        for name in w_dirs:
            action(name, j)

    loaded(wbuf.at[zh], 6)
    project(0)
    each(w_x2, 0)
    each(w_x2, 1)
    a_relay(0)
    each(w_x2, 2)
    a_relay(1)
    each(w_x3, 0)
    a_relay(2)
    each(w_x3, 1)
    each(w_x3, 2)
    a_relay(3)
    w_x4()
    for half in range(2):
        project(-1, half)
        project(1, half)
        y_partial(half)
    y_sum(0)
    y_sum(1)

    for sent, sem in ((kv.at[pl.ds(0, count[0])], kv_send), (wbuf.at[pl.ds(0, 3)], w_send),
                      (abuf.at[pl.ds(0, 3)], a_send), (ysend, y_send)):
        remote(sent, sent, sem, kv_recv.at[0, 0, 0], "s").wait_send()


def body(queries, keys, values, out_weight, storm_mask):
    rows, width = queries.shape
    anywhere = pl.BlockSpec(memory_space=pl.ANY)
    dma = pltpu.SemaphoreType.DMA
    return pl.pallas_call(
        kernel,
        out_shape=jax.ShapeDtypeStruct((rows, 512), BF16),
        in_specs=[anywhere, anywhere, anywhere, anywhere, anywhere],
        out_specs=pl.BlockSpec(memory_space=pltpu.VMEM),
        scratch_shapes=[
            pltpu.SMEM(storm_mask.shape, jnp.int32),
            pltpu.VMEM((512, HDIM), BF16),
            pltpu.VMEM((256, SUB, HDIM), BF16),
            pltpu.VMEM((4, 4, 256, 512), BF16),
            pltpu.VMEM((4, 2, BLOCK, 256), BF16),
            pltpu.VMEM((512, HDIM), F32),
            pltpu.VMEM((512, 256), F32),
            pltpu.VMEM((2, 3, BLOCK, 512), BF16),
            pltpu.VMEM((2, 3, BLOCK, 512), BF16),
            pltpu.VMEM((4, 256, 512), F32),
            dma((7,)), dma, dma((4, 4, 4)), dma((4, 4)),
            dma, dma((6,)), dma((6, 3)), dma,
            dma, dma((4, 3)), dma, dma((2, 3)),
        ],
        compiler_params=pltpu.CompilerParams(
            collective_id=0, has_side_effects=True, vmem_limit_bytes=56 * 1024 * 1024),
    )(queries, keys, values, out_weight, storm_mask)


def solution(mesh):
    placed = (P("ctx", "tp"), P("ctx", None), P("ctx", None), P("tp", None), P())
    return jax.shard_map(
        body, mesh=mesh, in_specs=placed, out_specs=P("ctx", "tp"), check_vma=False
    )
```

time: 658 us -> 84 us (0.13)
  waiting for transfers between devices: 577 us -> 0 us
  Pallas kernels: 0 us -> 82.2 us
  matrix products: 24.8 us -> 0 us
  loops' own time: 21.1 us -> 0 us
  between operations: 13.2 us -> 0.01 us
  local copies, waits for them, and re-layouts: 13.9 us -> 1.67 us
    psum x1 -> x0, waiting for transfers between devices: 443 us -> none  [body(): lax.psum(jnp.dot(attended, out_weight, preferred_element_type=jnp.float32...]
    all_gather x2 -> x0, waiting for transfers between devices: 134 us -> none  [the longest x1 68.1 us: body(): keys_part = lax.all_gather(local_keys, 'ctx', axis=0, tiled=True)]
    pallas_call x0 -> x1, Pallas kernels: none -> 82.2 us  [body(): pl.pallas_call(kernel, out_shape=jax.ShapeDtypeStruct((rows, 512), BF16),...]
    dot_general x20 -> x0, matrix products: 24.8 us -> none  [the longest x16 15.7 us: update(): allowed = jnp.dot(row_mask, one_hot) > 0.5]
    another operation x17 -> x0, loops' own time: 21.1 us -> none  [the longest x1 20.9 us: body(): carry, unused = lax.scan(inner, carry, jnp.arange(count // stride))]
    dynamic_slice x18 -> x0, local copies, waits for them, and re-layouts: 11.5 us -> none  [the longest x16 9.38 us: body(): carry, unused = lax.scan(inner, carry, jnp.arange(count // stride))]
  transfers between devices with their start and end apart: 3 -> 0, of which waited for: 3 -> 0; matrix products, arithmetic and copies ran while one was open for 1% -> 0% of each run, Pallas kernels for 0% -> 0%
where the time goes in v2:
time: 84 us; the launch traced here: 83.9 us
  Pallas kernels  82.2 us (98%)
  local copies, waits for them, and re-layouts  1.67 us (2%)
    pallas_call x1, Pallas kernels, body(): pl.pallas_call(kernel, out_shape=jax.ShapeDtypeStruct((rows, 512), BF16),...  82.2 us

profile of v2, /device:TPU:1, one launch (start us, length us, event | category | flops | bytes accessed | tf_op | source)
XLA Modules:
  0.0 83.9 jit_solution(14761646766592893746)
XLA Ops:
  0.0 82.2 %shard_map.55 = bf16[256,512]{1,0:T(8,128)(2,1)} custom-call(bf16[256,256]{1,0:T(8,128)(2,1)} %q_hbm.1, bf16[256,512]{1,0:T(8,128)(2,1)} %k_hbm.1, bf16[256,512]{1,0:T(8,128)(2,1)} %v_hbm.1, bf16[256,8192]{1,0:T(8,128)(2,1)} %w_hbm.1, s32[64,64]{1,0:T(8,128)} %mask_hbm.1), custom_call_target="tpu_custom_call" | custom-call | tf_op jit(solution)/shard_map/pallas_call | solution.py:381
  82.2 1.7 %copy.7 = bf16[256,512]{1,0:T(8,128)(2,1)} copy(bf16[256,512]{1,0:T(8,128)(2,1)} %shard_map.55) | data formatting | bytes 524288

commit v3 on v2

--- a/solution.py
+++ b/solution.py
@@ -34,6 +34,7 @@
 FIRST = (0, 1, 0, 1)
 SUB = 64
 W_SLOTS = (1, 3, 5, 7, 10, 13)
+W_ACROSS = (14, 15)
 W_EARLY = 3
 
 
@@ -100,7 +101,16 @@
     pl.semaphore_wait(barrier, len(devices))
 
     shift = {"x+": (-1, 0), "x-": (1, 0), "x2": (2, 0), "z+": (0, -1), "z-": (0, 1), "z2": (0, 2)}
-    count = [0]
+    count = [0] * 4
+
+    def at(places, action):
+        if len(places) == 4:
+            action()
+        elif places:
+            here = x == places[0]
+            for place in places[1:]:
+                here = here | (x == place)
+            pl.when(here)(action)
 
     def kv_ref(sub, dx, dz, part):
         first = kv_at(group_of(dx, dz), core, sub)
@@ -108,7 +118,6 @@
 
     def kv_forward(sub, dx, dz, part, to):
         ref = kv_ref(sub, dx, dz, part)
-        count[0] += 2 if part is None else 1
         if to == "s":
             rsem = kv_sib.at[dx % 4, dz % 4]
         else:
@@ -119,23 +128,48 @@
     def kv_handle(sub, dx, dz):
         along = (dx, dz) if FIRST[sub] == 0 else (dz, dx)
         one, two = ("x", "z") if FIRST[sub] == 0 else ("z", "x")
-        if (dx, dz) == (0, 0):
-            loaded(kv_ref(sub, 0, 0, None), sub)
-        else:
+        wanted = [v for v in range(4) if (v + dx) % 4 <= v]
+        held = sorted(set(wanted) | ({0} if FIRST[sub] == 1 and dx == 1 else set()))
+        forwards = []
+
+        def forward(part, to):
+            places = wanted
+            if to[0] == "x":
+                move = {"+": 1, "-": -1, "2": 2}[to[1]]
+                places = [v for v in held if (v + dx) % 4 <= (v + move) % 4
+                          or (v == 1 and dx == 0 and move == -1 and FIRST[sub] == 1)]
+            for v in places:
+                count[v] += 2 if part is None else 1
+            if forwards and forwards[-1][0] == places:
+                forwards[-1][1].append((part, to))
+            else:
+                forwards.append((places, [(part, to)]))
+
+        def arrive():
             ref = kv_ref(sub, dx, dz, None)
-            remote(ref, ref, kv_send, kv_recv.at[sub, dx % 4, dz % 4], "s").wait_recv()
+            if (dx, dz) == (0, 0):
+                loaded(ref, sub)
+            else:
+                remote(ref, ref, kv_send, kv_recv.at[sub, dx % 4, dz % 4], "s").wait_recv()
+
         if along[1] == 0:
             if along[0] == 0:
-                kv_forward(sub, dx, dz, None, one + "+")
-                kv_forward(sub, dx, dz, None, one + "-")
-                kv_forward(sub, dx, dz, None, one + "2")
-            kv_forward(sub, dx, dz, None, two + "+")
-            kv_forward(sub, dx, dz, None, two + "-")
+                for sign in "+-2":
+                    forward(None, one + sign)
+            forward(None, two + "+")
+            forward(None, two + "-")
         elif along[1] == -1:
-            kv_forward(sub, dx, dz, 0, two + "+")
+            forward(0, two + "+")
         elif along[1] == 1:
-            kv_forward(sub, dx, dz, 1, two + "-")
-        kv_forward(sub, dx, dz, None, "s")
+            forward(1, two + "-")
+        forward(None, "s")
+        at(held, arrive)
+        for places, which in forwards:
+            def start():
+                for part, to in which:
+                    kv_forward(sub, dx, dz, part, to)
+
+            at(places, start)
 
     row0 = core * 128
     w_dirs = {"+": (1, ((1, 0), (1, 64), (2, 0))), "-": (-1, ((1, 0), (1, 64), (2, 64)))}
@@ -224,6 +258,10 @@
     def w_x4():
         ref = wbuf.at[pl.ds(0, 3), pl.ds(0, 2)]
         remote(ref, ref, w_send, wx_sib, "s").wait_recv()
+
+    def each(action, j):
+        for name in w_dirs:
+            action(name, j)
 
     m_ref[...] = jnp.full(m_ref.shape, -1e30, F32)
     acc_ref[...] = jnp.zeros(acc_ref.shape, F32)
@@ -257,13 +295,13 @@
                 value = value + jnp.where(number == e, offset[axis] % 4, 0)
         return value
 
+    w_first()
     for sub in range(4):
         kv_handle(sub, 0, 0)
-    w_first()
 
     def step(i, carry):
         for e, (_, pieces) in enumerate(PROGRAM):
-            if pieces or e in W_SLOTS:
+            if pieces or e in W_SLOTS or e in W_ACROSS:
                 @pl.when(i == e)
                 def _():
                     for piece in pieces:
@@ -272,11 +310,16 @@
                         if W_SLOTS.index(e) == W_EARLY:
                             w_x1_early()
                         w_slot(W_SLOTS.index(e), then=W_SLOTS.index(e) >= W_EARLY)
+                    if e in W_ACROSS:
+                        each(w_x2, W_ACROSS.index(e))
 
         dx, dz = pick(i, 0), pick(i, 1)
         group = ((x + dx) % 4) * 4 + (zl + dz) % 4
-        ref = kv.at[pl.ds(kv_at(group, 1 - core, 0), 8)]
-        remote(ref, ref, kv_send, kv_sib.at[dx, dz], "s").wait_recv()
+
+        @pl.when((x + dx) % 4 <= x)
+        def _():
+            ref = kv.at[pl.ds(kv_at(group, 1 - core, 0), 8)]
+            remote(ref, ref, kv_send, kv_sib.at[dx, dz], "s").wait_recv()
 
         @pl.when(group <= own_group)
         def _():
@@ -345,21 +388,15 @@
             result = result + yin[half, n].astype(F32)
         out_ref[rows] = result.astype(BF16)
 
-    def each(action, j):
-        for name in w_dirs:
-            action(name, j)
-
     loaded(wbuf.at[zh], 6)
     project(0)
-    each(w_x2, 0)
-    each(w_x2, 1)
+    each(w_x2, 2)
+    each(w_x3, 0)
     a_relay(0)
-    each(w_x2, 2)
+    each(w_x3, 1)
     a_relay(1)
-    each(w_x3, 0)
+    each(w_x3, 2)
     a_relay(2)
-    each(w_x3, 1)
-    each(w_x3, 2)
     a_relay(3)
     w_x4()
     for half in range(2):
@@ -369,7 +406,13 @@
     y_sum(0)
     y_sum(1)
 
-    for sent, sem in ((kv.at[pl.ds(0, count[0])], kv_send), (wbuf.at[pl.ds(0, 3)], w_send),
+    for v in range(4):
+        def sent_kv():
+            sent = kv.at[pl.ds(0, count[v])]
+            remote(sent, sent, kv_send, kv_recv.at[0, 0, 0], "s").wait_send()
+
+        at([v], sent_kv)
+    for sent, sem in ((wbuf.at[pl.ds(0, 3)], w_send),
                       (abuf.at[pl.ds(0, 3)], a_send), (ysend, y_send)):
         remote(sent, sent, sem, kv_recv.at[0, 0, 0], "s").wait_send()
 

time: 84 us -> 81.8 us (0.974)
  the two profiles are of different devices: /device:TPU:1 before, /device:TPU:4 now
where the time goes in v3:
time: 81.8 us; the launch traced here: 81.6 us
  Pallas kernels  80 us (98%)
  local copies, waits for them, and re-layouts  1.67 us (2%)
    pallas_call x1, Pallas kernels, body(): pl.pallas_call(kernel, out_shape=jax.ShapeDtypeStruct((rows, 512), BF16),...  80 us
    unnamed x1, local copies, waits for them, and re-layouts  1.67 us

profile of v3, /device:TPU:4, one launch (start us, length us, event | category | flops | bytes accessed | tf_op | source)
XLA Modules:
  0.0 81.6 jit_solution(6279887745257603276)
XLA Ops:
  0.0 80.0 %shard_map.55 = bf16[256,512]{1,0:T(8,128)(2,1)} custom-call(bf16[256,256]{1,0:T(8,128)(2,1)} %q_hbm.1, bf16[256,512]{1,0:T(8,128)(2,1)} %k_hbm.1, bf16[256,512]{1,0:T(8,128)(2,1)} %v_hbm.1, bf16[256,8192]{1,0:T(8,128)(2,1)} %w_hbm.1, s32[64,64]{1,0:T(8,128)} %mask_hbm.1), custom_call_target="tpu_custom_call" | custom-call | tf_op jit(solution)/shard_map/pallas_call | solution.py:424
  80.0 1.7 %copy.7 = bf16[256,512]{1,0:T(8,128)(2,1)} copy(bf16[256,512]{1,0:T(8,128)(2,1)} %shard_map.55) | data formatting | bytes 524288
